TPU v7x, 256 devices: a whole 4x4x8 slice. The times are simulated.
256 devices in a mesh: lat: 8 (over z_lo, core), lon: 8 (over z_hi, x), chan: 4 (over y).
Axes of the slice: x: 4, y: 4, z: 8 (z_hi: 2, z_lo: 4; z = z_hi * 4 + z_lo), core: 2. Of those that a mesh axis runs over, the one named last changes fastest.
Arguments:
- queries: bfloat16 [128, 64, 2560], P('lat', 'lon', 'chan'), may hold values from -8 to 8
- keys: bfloat16 [128, 64, 2560], P('lat', 'lon', 'chan'), may hold values from -8 to 8
- values: bfloat16 [128, 64, 2560], P('lat', 'lon', 'chan'), may hold values from -6 to 6
- attn_out: bfloat16 [128, 64, 2560], P('lat', 'lon', 'chan'), may hold values from -6 to 6
- grad_out: bfloat16 [128, 64, 5120], P('lat', 'lon', 'chan'), may hold values from -6 to 6
- w_out: bfloat16 [5120, 2560], P(('lat', 'lon'), 'chan'), may hold values from -0.078125 to 0.078125
- bias_table: float32 [20, 25, 13], P('chan'), may hold values from -5 to 5
- key_mask: int32 [128, 64], replicated, may hold values 0 or 1
Outputs:
- grad_queries: bfloat16 [128, 64, 2560], P('lat', 'lon', 'chan')
- grad_keys: bfloat16 [128, 64, 2560], P('lat', 'lon', 'chan')
- grad_values: bfloat16 [128, 64, 2560], P('lat', 'lon', 'chan')
- grad_wout: float32 [5120, 2560], P(('lat', 'lon'), 'chan')
- grad_table: float32 [20, 25, 13], P('chan')
All inputs are finite; a program needn't handle non-finite values.
Results may differ from a plain program's by a relative error of at most 0.007.
Values may be sent and summed in bfloat16 or wider, within the bound.
No kernel may reach another device: no remote copies, remote signals or barrier semaphores. Data moves between devices by JAX's collectives and lax.ppermute only.
A program may use at most 128 MiB of HBM per device.

v0:
```python
import jax
import jax.numpy as jnp
from jax import lax
from jax.sharding import PartitionSpec as P

HEAD_DIM = 128
WIN = 13


def extended_2(value, sides, width, wrap):
    for axis, dim in sides:
        count, length = (lax.axis_size(axis), value.shape[dim])
        up = [(i, (i + 1) % count) for i in range(count if wrap else count - 1)]
        down = [(j, i) for i, j in up]
        last = lax.slice_in_dim(value, length - width, length, axis=dim)
        leading = lax.slice_in_dim(value, 0, width, axis=dim)
        before = lax.ppermute(last, axis, up)
        after = lax.ppermute(leading, axis, down)
        value = jnp.concatenate([before, value, after], axis=dim)
    return value


def fold_lon(extended, core_width):
    full_width = extended.shape[2]
    reach_cells = (full_width - core_width) // 2
    rim_cells = jnp.concatenate(
        [extended[:, :, :reach_cells], extended[:, :, full_width - reach_cells :]], axis=2
    )
    received = extended_2(rim_cells.astype(jnp.bfloat16), (("lon", 2),), reach_cells, True).astype(
        rim_cells.dtype
    )
    middle = extended[:, :, reach_cells : full_width - reach_cells]
    front_add = jnp.pad(
        received[:, :, :reach_cells], ((0, 0), (0, 0), (0, core_width - reach_cells), (0, 0))
    )
    back_add = jnp.pad(
        received[:, :, 3 * reach_cells :], ((0, 0), (0, 0), (core_width - reach_cells, 0), (0, 0))
    )
    return middle + front_add + back_add


def fold_lat(extended, core_width):
    full_width = extended.shape[1]
    reach_cells = (full_width - core_width) // 2
    rim_cells = jnp.concatenate(
        [extended[:, :reach_cells], extended[:, full_width - reach_cells :]], axis=1
    )
    received = extended_2(rim_cells.astype(jnp.bfloat16), (("lat", 1),), reach_cells, False).astype(
        rim_cells.dtype
    )
    middle = extended[:, reach_cells : full_width - reach_cells]
    front_add = jnp.pad(
        received[:, :reach_cells], ((0, 0), (0, core_width - reach_cells), (0, 0), (0, 0))
    )
    back_add = jnp.pad(
        received[:, 3 * reach_cells :], ((0, 0), (core_width - reach_cells, 0), (0, 0), (0, 0))
    )
    return middle + front_add + back_add


def local(queries, keys, values, attn_out, grad_out, w_out, bias_table, key_mask):
    lat_rows, lon_cols, chan_width = queries.shape
    head_count = bias_table.shape[0]
    reach_cells = WIN // 2
    score_scale = HEAD_DIM ** (-0.5)
    tokens = lat_rows * lon_cols
    ext_rows = lat_rows + 2 * reach_cells
    ext_cols = lon_cols + 2 * reach_cells
    row_block = 4
    key_span = row_block + WIN - 1
    block_count = lat_rows // row_block
    block_rows = row_block * lon_cols
    block_keys = key_span * ext_cols
    offset_rows = 2 * WIN - 1
    low_pad = row_block - 1
    lat_total = lat_rows * lax.axis_size("lat")
    lon_total = lon_cols * lax.axis_size("lon")
    contract_lead = (((0,), (0,)), ((), ()))
    full_grad = lax.all_gather(grad_out, "chan", axis=2, tiled=True).reshape(tokens, -1)
    grad_cols = jnp.transpose(full_grad)
    slab_part = grad_cols
    grad_attn = lax.dot_general(
        slab_part,
        lax.all_gather(w_out, ("lat", "lon"), axis=0, tiled=True),
        contract_lead,
        preferred_element_type=jnp.float32,
    ).astype(jnp.bfloat16)
    kv_pair = jnp.stack([keys, values])
    extended = extended_2(kv_pair, (("lat", 1), ("lon", 2)), reach_cells, True)
    lat_first = lax.axis_index("lat") * lat_rows
    lon_first = lax.axis_index("lon") * lon_cols
    ext_col = lon_first - reach_cells + jnp.arange(ext_cols, dtype=jnp.int32)
    wrap_col = ext_col % lon_total
    mask_cols = jnp.take(key_mask, wrap_col, axis=1)
    mark_cols = wrap_col % 4 == 0
    rel_lon = (
        jnp.arange(ext_cols, dtype=jnp.int32)[None, :]
        - jnp.arange(lon_cols, dtype=jnp.int32)[:, None]
    )
    in_lon = (rel_lon >= 0) & (rel_lon < WIN)
    lon_pick = jnp.clip(rel_lon, 0, WIN - 1)
    lon_table = jnp.take(bias_table, lon_pick, axis=2).transpose(0, 2, 1, 3)
    table_pad = jnp.pad(lon_table, ((0, 0), (0, 0), (low_pad, low_pad), (0, 0)))
    query_heads = queries.reshape(lat_rows, lon_cols, head_count, HEAD_DIM)
    grad_heads = grad_attn.reshape(lat_rows, lon_cols, head_count, HEAD_DIM)

    def block_step(state_pair, block_index):
        grad_pair, table_acc = state_pair
        local_first = block_index * row_block
        top_row = lat_first + local_first
        key_first = jnp.clip(top_row - reach_cells, 0, lat_total - key_span)
        key_local = key_first - (lat_first - reach_cells)
        query_rows = top_row + jnp.arange(row_block, dtype=jnp.int32)
        window_first = jnp.clip(query_rows - reach_cells, 0, lat_total - WIN)
        key_glob = key_first + jnp.arange(key_span, dtype=jnp.int32)
        in_lat = (key_glob[None, :] >= window_first[:, None]) & (
            key_glob[None, :] < window_first[:, None] + WIN
        )
        mask_rows = lax.dynamic_slice_in_dim(mask_cols, key_first, key_span, 0)
        valid_keys = (mask_rows == 1) | (key_glob % 4 == 0)[:, None] & mark_cols[None, :]
        allowed = in_lat[:, None, :, None] & in_lon[None, :, None, :] & valid_keys[None, None, :, :]
        allowed = allowed.reshape(block_rows, block_keys)
        shifts = key_first - query_rows + (WIN - 1) + low_pad
        bias_parts = [
            lax.dynamic_slice_in_dim(table_pad, shifts[row_pos], key_span, 2)
            for row_pos in range(row_block)
        ]
        bias_rows = jnp.stack(bias_parts, axis=1).reshape(head_count, block_rows, block_keys)
        query_block = lax.dynamic_slice_in_dim(query_heads, local_first, row_block, 0).reshape(
            block_rows, head_count, HEAD_DIM
        )
        grad_block = lax.dynamic_slice_in_dim(grad_heads, local_first, row_block, 0).reshape(
            block_rows, head_count, HEAD_DIM
        )
        pair_block = lax.dynamic_slice_in_dim(extended, key_local, key_span, 1).reshape(
            2, block_keys, head_count, HEAD_DIM
        )
        key_block = pair_block[0]
        value_block = pair_block[1]
        scores = (
            score_scale
            * jnp.einsum("qhd,khd->hqk", query_block, key_block, preferred_element_type=jnp.float32)
            + bias_rows
        )
        scores = jnp.where(allowed[None], scores, -1e30)
        row_max = jnp.max(scores, axis=2, keepdims=True)
        weights_exp = jnp.exp(scores - row_max)
        prob_rows = weights_exp / jnp.sum(weights_exp, axis=2, keepdims=True)
        grad_prob = jnp.einsum(
            "qhd,khd->hqk", grad_block, value_block, preferred_element_type=jnp.float32
        )
        row_delta = jnp.sum(prob_rows * grad_prob, axis=2, keepdims=True)
        dscore = prob_rows * (grad_prob - row_delta)
        score_grid = dscore.reshape(head_count, row_block, lon_cols, key_span, ext_cols)
        score_grid = score_grid.transpose(0, 1, 3, 2, 4).reshape(
            head_count, row_block, key_span, lon_cols * ext_cols
        )
        for row_pos in range(row_block):
            prior_sum = lax.dynamic_slice_in_dim(table_acc, shifts[row_pos], key_span, 1)
            table_acc = lax.dynamic_update_slice_in_dim(
                table_acc, prior_sum + score_grid[:, row_pos], shifts[row_pos], 1
            )
        dscore_low = dscore.astype(jnp.bfloat16)
        prob_low = prob_rows.astype(jnp.bfloat16)
        grad_query = (
            score_scale
            * jnp.einsum("hqk,khd->qhd", dscore_low, key_block, preferred_element_type=jnp.float32)
        ).astype(jnp.bfloat16)
        key_part = score_scale * jnp.einsum(
            "hqk,qhd->khd", dscore_low, query_block, preferred_element_type=jnp.float32
        )
        value_part = jnp.einsum(
            "hqk,qhd->khd", prob_low, grad_block, preferred_element_type=jnp.float32
        )
        new_part = jnp.stack([key_part, value_part]).reshape(2, key_span, ext_cols, chan_width)
        prior_pair = lax.dynamic_slice_in_dim(grad_pair, key_local, key_span, 1)
        grad_pair = lax.dynamic_update_slice_in_dim(grad_pair, prior_pair + new_part, key_local, 1)
        return ((grad_pair, table_acc), grad_query)

    zero_pair = jnp.zeros((2, ext_rows, ext_cols, chan_width), jnp.float32)
    zero_table = jnp.zeros(
        (head_count, offset_rows + 2 * low_pad, lon_cols * ext_cols), jnp.float32
    )
    (grad_pair, table_acc), query_blocks = lax.scan(
        block_step, (zero_pair, zero_table), jnp.arange(block_count, dtype=jnp.int32)
    )
    grad_queries = query_blocks.reshape(lat_rows, lon_cols, chan_width)
    table_core = table_acc[:, low_pad : low_pad + offset_rows].reshape(
        head_count, offset_rows, lon_cols, ext_cols
    )
    col_take = (
        jnp.arange(lon_cols, dtype=jnp.int32)[:, None] + jnp.arange(WIN, dtype=jnp.int32)[None, :]
    )
    col_take = jnp.broadcast_to(
        col_take[None, None, :, :], (head_count, offset_rows, lon_cols, WIN)
    )
    table_local = jnp.sum(jnp.take_along_axis(table_core, col_take, axis=3), axis=2)
    grad_table = lax.psum(table_local, ("lat", "lon"))
    folded = fold_lat(fold_lon(grad_pair, lon_cols), lat_rows)
    grad_keys = folded[0].astype(jnp.bfloat16)
    grad_values = folded[1].astype(jnp.bfloat16)
    saved_out = attn_out.reshape(tokens, chan_width)
    slab_part = grad_cols
    grad_wout = lax.psum_scatter(
        jnp.dot(slab_part, saved_out, preferred_element_type=jnp.float32),
        ("lat", "lon"),
        scatter_dimension=0,
        tiled=True,
    )
    return (grad_queries, grad_keys, grad_values, grad_wout, grad_table)


def solution(mesh):
    return jax.shard_map(
        local,
        mesh=mesh,
        in_specs=(
            P("lat", "lon", "chan"),
            P("lat", "lon", "chan"),
            P("lat", "lon", "chan"),
            P("lat", "lon", "chan"),
            P("lat", "lon", "chan"),
            P(("lat", "lon"), "chan"),
            P("chan", None, None),
            P(),
        ),
        out_specs=(
            P("lat", "lon", "chan"),
            P("lat", "lon", "chan"),
            P("lat", "lon", "chan"),
            P(("lat", "lon"), "chan"),
            P("chan", None, None),
        ),
        check_vma=False,
    )
```

profile of v0, /device:TPU:240, one launch (start us, length us, event | category | flops | bytes accessed | tf_op | source)
XLA Modules:
  0.0 933.4 jit_solution(14924076082434811027)
XLA Ops:
  7.2 1.8 copy.63
  9.8 26.9 %all-gather.3.cloned.1.call-done = bf16[16,8,5120]{2,0,1:T(8,128)(2,1)} async-done(((bf16[16,8,1280]{2,0,1:T(8,128)(2,1)}), bf16[16,8,5120]{2,0,1:T(8,128)(2,1)}) %all-gather.3.cloned.1.call-update) | async-done | bytes 1310736 | tf_op jit(solution)/shard_map/all_gather | solution.py:79
  36.7 7.9 convolution_bitcast_fusion.1
  44.7 0.9 copy-done.9
  45.8 1.7 collective-permute-start.1
  49.0 1.0 collective-permute-done
  51.5 4.6 collective-permute-start.3
  56.1 1.4 gather_fusion.1
  58.2 0.9 pad.20.clone
  59.1 11.4 %collective-permute-done.3 = bf16[2,28,6,640]{3,0,2,1:T(2,128)(2,1)S(1)} collective-permute-done((bf16[2,28,6,640]{3,0,2,1:T(2,128)(2,1)S(1)}, bf16[2,28,6,640]{3,0,2,1:T(2,128)(2,1)S(1)}, u32[]{:S(2)}, u32[]{:S(2)}) %collective-permute-start.3) | collective-permute-done | bytes 430112 | tf_op jit(solution)/shard_map/ppermute | solution.py:18
  70.6 10.3 %collective-permute-done.2 = bf16[2,28,6,640]{3,0,2,1:T(2,128)(2,1)S(1)} collective-permute-done((bf16[2,28,6,640]{3,0,2,1:T(2,128)(2,1)S(1)}, bf16[2,28,6,640]{3,0,2,1:T(2,128)(2,1)S(1)}, u32[]{:S(2)}, u32[]{:S(2)}) %collective-permute-start.2) | collective-permute-done | bytes 430112 | tf_op jit(solution)/shard_map/ppermute | solution.py:17
  80.9 2.1 pad_maximum_fusion.1
  83.0 156.4 %all-gather.5.cloned.1.call-done = bf16[5120,640]{1,0:T(8,128)(2,1)} async-done(((bf16[80,640]{1,0:T(8,128)(2,1)}), bf16[5120,640]{1,0:T(8,128)(2,1)}) %all-gather.5.cloned.1.call-update) | async-done | bytes 6553616 | tf_op jit(solution)/shard_map/all_gather | solution.py:84
  239.4 4.6 fusion.42
  244.0 1.9 broadcast_in_dim.94
  245.9 117.0 %while.18 = (s32[]{:T(128)}, f32[2,28,20,640]{3,2,1,0:T(8,128)}, f32[5,31,160]{2,1,0:T(8,128)S(1)}, bf16[4,32,5,128]{3,1,2,0:T(8,128)(2,1)}, s32[4]{0:T(128)S(1)...) while((s32[]{:T(128)}, f32[2,28,20,640]{3,2,1,0:T(8,128)}, ...), condition=%wide.region_4.5_spmd.clone, body=%wide.region_0.0_spmd.clone.sunk | while | flops 67648624 | bytes 32509632 | solution.py:184
  257.6 1.3 constant_dynamic-slice_fusion.7
  259.8 1.9 dynamic-slice_bitcast_fusion.5
  265.9 1.2 stack.66
  268.0 1.2 stack.67
  272.1 3.0 fusion.106
  286.8 1.3 constant_dynamic-slice_fusion.7
  289.0 1.9 dynamic-slice_bitcast_fusion.5
  295.2 1.2 stack.66
  297.2 1.2 stack.67
  301.4 3.0 fusion.106
  316.0 1.3 constant_dynamic-slice_fusion.7
  318.3 1.9 dynamic-slice_bitcast_fusion.5
  324.4 1.2 stack.66
  326.4 1.2 stack.67
  330.6 3.1 fusion.106
  345.3 1.3 constant_dynamic-slice_fusion.7
  347.5 1.9 dynamic-slice_bitcast_fusion.5
  353.6 1.2 stack.66
  355.7 1.2 stack.67
  359.8 3.1 fusion.106
  363.0 2.2 convert.16
  365.3 1.1 copy.70
  366.5 1.1 copy.71
  367.6 2.0 collective-permute-start.4
  370.2 0.9 reshape.332
  371.3 155.3 %gather_fusion.2 = f32[13000]{0:T(1024)S(1)} fusion(f32[5,25,8,20]{3,2,1,0:T(8,128)S(1)} %reshape.333, s32[13000]{0:T(1024)S(1)} %reshape.350), kind=kCustom, calls=%fused_computation.2 | custom fusion | bytes 312000 | tf_op jit(solution)/shard_map/jit(take_along_axis)/gather | solution.py:197
  527.0 1.1 copy.73
  528.1 1.1 copy.72
  529.9 2.3 fusion.59
  532.3 2.1 collective-permute-start.6
  534.3 4.4 collective-permute-start.7
  539.0 386.1 %psum.7 = f32[5,25,13]{2,1,0:T(8,128)S(1)} all-reduce(f32[5,25,13]{2,1,0:T(8,128)S(1)} %select_reduce_fusion), channel_id=1, replica_groups=mesh['lat'=8,'lon'=8,'chan'=4] {'lat','lon'}, use_global_device_ids=true, to_apply=%region_7.8 | all-reduce | flops 1625 | bytes 13000 | tf_op jit(solution)/shard_map/psum | solution.py:198
  (281 shorter events, 57.6 us)
Async XLA Ops:
  7.2 29.5 %copy-start = (bf16[16,8,640]{2,1,0:T(8,128)(2,1)S(1)}, bf16[16,8,640]{2,1,0:T(8,128)(2,1)}, u32[]{:S(2)}) copy-start(bf16[16,8,640]{2,1,0:T(8,128)(2,1)} %param.13) | copy-start | bytes 491524
  7.2 29.5 %all-gather.3.cloned.1.call-start = ((), (), s32[]{:S(2)}) async-start(), calls=%async_computation.1 | async-start | bytes 1638400 | tf_op jit(solution)/shard_map/all_gather | solution.py:79
  9.0 230.4 %all-gather.5.cloned.1.call-start = ((), (), s32[]{:S(2)}) async-start(), calls=%async_computation.2 | async-start | bytes 6656000 | tf_op jit(solution)/shard_map/all_gather | solution.py:84
  9.8 917.1 %reduce-scatter.2.cloned.1.call-start = ((), (), s32[]{:S(2)}) async-start(), calls=%async_computation.3 | async-start | bytes 13312000 | tf_op jit(solution)/shard_map/reduce_scatter | solution.py:204
  44.6 0.9 copy-start.9
  44.6 1.0 copy-start.10
  44.6 3.0 copy-start.8
  45.7 4.4 collective-permute-start
  45.8 4.8 collective-permute-start.1
  50.6 5.5 copy-start.1
  51.5 19.0 %collective-permute-start.3 = (bf16[2,28,6,640]{3,0,2,1:T(2,128)(2,1)S(1)}, bf16[2,28,6,640]{3,0,2,1:T(2,128)(2,1)S(1)}, u32[]{:S(2)}, u32[]{:S(2)}) collective-permute-start(bf16[2,28,6,640]{3,0,2,1:T(2,128)(2,1)S(1)} %copy.59), channel_id=1, source_target_pairs={{4,0},{8,4},{12,8},{16,12},{20,16},{24,20},{28,24},{0,28},{5,1},{9... | collective-permute-start | bytes 1290248 | tf_op jit(solution)/shard_map/ppermute | solution.py:18
  56.1 24.7 %collective-permute-start.2 = (bf16[2,28,6,640]{3,0,2,1:T(2,128)(2,1)S(1)}, bf16[2,28,6,640]{3,0,2,1:T(2,128)(2,1)S(1)}, u32[]{:S(2)}, u32[]{:S(2)}) collective-permute-start(bf16[2,28,6,640]{3,0,2,1:T(2,128)(2,1)S(1)} %copy.58), channel_id=1, source_target_pairs={{0,4},{4,8},{8,12},{12,16},{16,20},{20,24},{24,28},{28,0},{1,5},{5... | collective-permute-start | bytes 1290248 | tf_op jit(solution)/shard_map/ppermute | solution.py:17
  80.9 158.5 %copy-start.11 = (bf16[16,8,5120]{2,0,1:T(8,128)(2,1)S(1)}, bf16[16,8,5120]{2,0,1:T(8,128)(2,1)}, u32[]{:S(2)}) copy-start(bf16[16,8,5120]{2,0,1:T(8,128)(2,1)} %all-gather.3.cloned.1.call-done) | copy-start | bytes 3932164
  245.9 13.4 %copy-start.12 = (bf16[16,8,5,128]{3,1,2,0:T(8,128)(2,1)}, bf16[16,8,5,128]{3,1,2,0:T(8,128)(2,1)S(1)}, u32[]{:S(2)}) copy-start(bf16[16,8,5,128]{3,1,2,0:T(8,128)(2,1)S(1)} %get-tuple-element.541) | copy-start | bytes 491524 | tf_op jit(solution)/shard_map/while
  270.5 1.5 copy-start.2
  270.9 1.3 copy-start.3
  272.1 3.0 copy-start.13
  275.2 13.4 %copy-start.12 = (bf16[16,8,5,128]{3,1,2,0:T(8,128)(2,1)}, bf16[16,8,5,128]{3,1,2,0:T(8,128)(2,1)S(1)}, u32[]{:S(2)}) copy-start(bf16[16,8,5,128]{3,1,2,0:T(8,128)(2,1)S(1)} %get-tuple-element.541) | copy-start | bytes 491524 | tf_op jit(solution)/shard_map/while
  299.7 1.5 copy-start.2
  300.1 1.3 copy-start.3
  301.4 3.0 copy-start.13
  304.4 13.4 %copy-start.12 = (bf16[16,8,5,128]{3,1,2,0:T(8,128)(2,1)}, bf16[16,8,5,128]{3,1,2,0:T(8,128)(2,1)S(1)}, u32[]{:S(2)}) copy-start(bf16[16,8,5,128]{3,1,2,0:T(8,128)(2,1)S(1)} %get-tuple-element.541) | copy-start | bytes 491524 | tf_op jit(solution)/shard_map/while
  328.9 1.5 copy-start.2
  329.3 1.3 copy-start.3
  330.6 3.1 copy-start.13
  333.6 13.4 %copy-start.12 = (bf16[16,8,5,128]{3,1,2,0:T(8,128)(2,1)}, bf16[16,8,5,128]{3,1,2,0:T(8,128)(2,1)S(1)}, u32[]{:S(2)}) copy-start(bf16[16,8,5,128]{3,1,2,0:T(8,128)(2,1)S(1)} %get-tuple-element.541) | copy-start | bytes 491524 | tf_op jit(solution)/shard_map/while
  358.2 1.5 copy-start.2
  358.6 1.3 copy-start.3
  359.8 3.1 copy-start.13
  365.3 4.3 copy-start.4
  365.3 4.3 copy-start.6
  365.3 4.7 copy-start.14
  367.6 159.4 %collective-permute-start.5 = (bf16[2,28,6,640]{3,0,2,1:T(2,128)(2,1)}, bf16[2,28,6,640]{3,0,2,1:T(2,128)(2,1)}, u32[]{:S(2)}, u32[]{:S(2)}) collective-permute-start(bf16[2,28,6,640]{3,0,2,1:T(2,128)(2,1)} %copy.71), channel_id=1, source_target_pairs={{4,0},{8,4},{12,8},{16,12},{20,16},{24,20},{28,24},{0,28},{5,1},{9... | collective-permute-start | bytes 1290248 | tf_op jit(solution)/shard_map/ppermute | solution.py:18
  367.6 160.5 %collective-permute-start.4 = (bf16[2,28,6,640]{3,0,2,1:T(2,128)(2,1)}, bf16[2,28,6,640]{3,0,2,1:T(2,128)(2,1)}, u32[]{:S(2)}, u32[]{:S(2)}) collective-permute-start(bf16[2,28,6,640]{3,0,2,1:T(2,128)(2,1)} %copy.70), channel_id=1, source_target_pairs={{0,4},{4,8},{8,12},{12,16},{16,20},{20,24},{24,28},{28,0},{1,5},{5... | collective-permute-start | bytes 1290248 | tf_op jit(solution)/shard_map/ppermute | solution.py:17
  369.6 1.7 copy-start.19
  369.6 1.7 copy-start.15
  369.6 1.7 copy-start.17
  526.6 2.6 copy-start.5
  526.6 2.6 copy-start.7
  529.2 0.7 copy-start.21
  529.9 8.9 copy-start.16
  529.9 8.9 copy-start.18
  529.9 8.9 copy-start.20
  532.2 393.8 %copy-start.22 = (pred[16]{0:T(512)(128)(4,1)S(1)}, pred[16]{0:T(512)(128)(4,1)}, u32[]{:S(2)}) copy-start(pred[16]{0:T(512)(128)(4,1)} %constant.227.clone.1) | copy-start | bytes 52
  532.3 393.6 %collective-permute-start.6 = (bf16[2,6,8,640]{3,2,1,0:T(8,128)(2,1)S(1)}, bf16[2,6,8,640]{3,2,1,0:T(8,128)(2,1)S(1)}, u32[]{:S(2)}, u32[]{:S(2)}) collective-permute-start(bf16[2,6,8,640]{3,2,1,0:T(8,128)(2,1)S(1)} %get-tuple-element.361), channel_id=1, source_target_pairs={{0,32},{32,64},{64,96},{96,128},{128,160},{160,192},{192,224},{1,3... | collective-permute-start | bytes 368648 | tf_op jit(solution)/shard_map/ppermute | solution.py:17
  534.3 391.5 %collective-permute-start.7 = (bf16[2,6,8,640]{3,2,1,0:T(8,128)(2,1)S(1)}, bf16[2,6,8,640]{3,2,1,0:T(8,128)(2,1)S(1)}, u32[]{:S(2)}, u32[]{:S(2)}) collective-permute-start(bf16[2,6,8,640]{3,2,1,0:T(8,128)(2,1)S(1)} %get-tuple-element.362), channel_id=1, source_target_pairs={{32,0},{64,32},{96,64},{128,96},{160,128},{192,160},{224,192},{33,... | collective-permute-start | bytes 368648 | tf_op jit(solution)/shard_map/ppermute | solution.py:18
Sparse Core Ops, SparseCore 0:
  9.8 26.8 all-gather.2
  38.5 200.8 all-gather.4
  242.6 461.3 reduce-scatter.1
where the time goes:
time: 935 us; the launch traced here: 933 us
  blocking collectives  386 us (41%)
  local copies, waits for them, and re-layouts  227 us (24%)
  waiting for transfers between devices  207 us (22%)
  loops' own time  33.7 us (4%)
  other arithmetic  28.7 us (3%)
  matrix products  21.7 us (2%)
  starting transfers between devices  15.1 us (2%)
  between operations  14.2 us (2%)
    psum x1, blocking collectives, local(): grad_table = lax.psum(table_local, ('lat', 'lon'))  386 us
    all_gather x1, waiting for transfers between devices, local(): lax.all_gather(w_out, ('lat', 'lon'), axis=0, tiled=True)  156 us
    gather x3, local copies, waits for them, and re-layouts, local(): jnp.take_along_axis(table_core, col_take, axis=3)  156 us
    another operation x1, loops' own time, local(): lax.scan(block_step, (zero_pair, zero_table), jnp.arange(block_count, dty...  33.7 us
    all_gather x1, waiting for transfers between devices, local(): lax.all_gather(grad_out, 'chan', axis=2, tiled=True).reshape(tokens, -1)  26.9 us
  transfers between devices with their start and end apart: 11, of which 6 were waited for; matrix products, arithmetic and copies ran while one was open for 29% of the time, Pallas kernels for 0%

commit v1 on v0

--- a/solution.py
+++ b/solution.py
@@ -195,7 +195,7 @@
         col_take[None, None, :, :], (head_count, offset_rows, lon_cols, WIN)
     )
     table_local = jnp.sum(jnp.take_along_axis(table_core, col_take, axis=3), axis=2)
-    grad_table = lax.psum(table_local, ("lat", "lon"))
+    grad_table = lax.psum(lax.psum(table_local, "lon"), "lat")
     folded = fold_lat(fold_lon(grad_pair, lon_cols), lat_rows)
     grad_keys = folded[0].astype(jnp.bfloat16)
     grad_values = folded[1].astype(jnp.bfloat16)

time: 935 us -> 723 us (0.77)
  blocking collectives: 386 us -> 89.5 us
  waiting for transfers between devices: 207 us -> 287 us
    psum x1 -> x2, blocking collectives: 386 us -> 89.5 us  [local(): grad_table = lax.psum(lax.psum(table_local, 'lon'), 'lat')]
    reduce_scatter x1, waiting for transfers between devices: 0.01 us -> 78.8 us  [local(): lax.psum_scatter(jnp.dot(slab_part, saved_out, preferred_element_type=jnp...]
  transfers between devices with their start and end apart: 11 -> 11, of which waited for: 6 -> 7; matrix products, arithmetic and copies ran while one was open for 29% -> 38% of each run, Pallas kernels for 0% -> 0%
where the time goes in v1:
time: 723 us; the launch traced here: 716 us
  waiting for transfers between devices  287 us (40%)
  local copies, waits for them, and re-layouts  227 us (31%)
  blocking collectives  89.5 us (12%)
  loops' own time  33.9 us (5%)
  other arithmetic  28.8 us (4%)
  matrix products  21.7 us (3%)
  starting transfers between devices  14.2 us (2%)
  between operations  14.2 us (2%)
    all_gather x1, waiting for transfers between devices, local(): lax.all_gather(w_out, ('lat', 'lon'), axis=0, tiled=True)  157 us
    gather x3, local copies, waits for them, and re-layouts, local(): jnp.take_along_axis(table_core, col_take, axis=3)  156 us
    psum x2, blocking collectives, local(): grad_table = lax.psum(lax.psum(table_local, 'lon'), 'lat')  89.5 us
    reduce_scatter x1, waiting for transfers between devices, local(): lax.psum_scatter(jnp.dot(slab_part, saved_out, preferred_element_type=jnp...  78.8 us
    another operation x1, loops' own time, local(): lax.scan(block_step, (zero_pair, zero_table), jnp.arange(block_count, dty...  33.9 us
    all_gather x1, waiting for transfers between devices, local(): lax.all_gather(grad_out, 'chan', axis=2, tiled=True).reshape(tokens, -1)  26.9 us
  transfers between devices with their start and end apart: 11, of which 7 were waited for; matrix products, arithmetic and copies ran while one was open for 38% of the time, Pallas kernels for 0%

profile of v1, /device:TPU:240, one launch (start us, length us, event | category | flops | bytes accessed | tf_op | source)
XLA Modules:
  0.0 716.0 jit_solution(15265825217043670548)
XLA Ops:
  7.2 1.8 copy.63
  9.8 26.9 %all-gather.3.cloned.1.call-done = bf16[16,8,5120]{2,0,1:T(8,128)(2,1)} async-done(((bf16[16,8,1280]{2,0,1:T(8,128)(2,1)}), bf16[16,8,5120]{2,0,1:T(8,128)(2,1)}) %all-gather.3.cloned.1.call-update) | async-done | bytes 1310736 | tf_op jit(solution)/shard_map/all_gather | solution.py:79
  36.7 7.9 %convolution_bitcast_fusion.1 = f32[5120,640]{1,0:T(8,128)} fusion(bf16[16,8,5120]{2,0,1:T(8,128)(2,1)} %all-gather.3.cloned.1.call-done, bf16[16,8,640]{2,1,0:T(8,128)(2,1)S(1)} %copy-done), kind=kOutput, calls=%fused_computation.77 | convolution fusion | flops 838860800 | bytes 14581760 | tf_op jit(solution)/shard_map/dot_general | solution.py:205
  45.8 1.7 collective-permute-start.1
  49.0 1.0 collective-permute-done
  51.5 4.6 collective-permute-start.3
  56.2 1.4 gather_fusion.1
  58.2 0.9 pad.20.clone
  59.1 11.3 %collective-permute-done.3 = bf16[2,28,6,640]{3,0,2,1:T(2,128)(2,1)S(1)} collective-permute-done((bf16[2,28,6,640]{3,0,2,1:T(2,128)(2,1)S(1)}, bf16[2,28,6,640]{3,0,2,1:T(2,128)(2,1)S(1)}, u32[]{:S(2)}, u32[]{:S(2)}) %collective-permute-start.3) | collective-permute-done | bytes 430112 | tf_op jit(solution)/shard_map/ppermute | solution.py:18
  70.5 10.5 %collective-permute-done.2 = bf16[2,28,6,640]{3,0,2,1:T(2,128)(2,1)S(1)} collective-permute-done((bf16[2,28,6,640]{3,0,2,1:T(2,128)(2,1)S(1)}, bf16[2,28,6,640]{3,0,2,1:T(2,128)(2,1)S(1)}, u32[]{:S(2)}, u32[]{:S(2)}) %collective-permute-start.2) | collective-permute-done | bytes 430112 | tf_op jit(solution)/shard_map/ppermute | solution.py:17
  81.0 2.1 pad_maximum_fusion.1
  83.1 157.3 %all-gather.5.cloned.1.call-done = bf16[5120,640]{1,0:T(8,128)(2,1)} async-done(((bf16[80,640]{1,0:T(8,128)(2,1)}), bf16[5120,640]{1,0:T(8,128)(2,1)}) %all-gather.5.cloned.1.call-update) | async-done | bytes 6553616 | tf_op jit(solution)/shard_map/all_gather | solution.py:84
  240.4 4.6 fusion.42
  245.0 1.9 broadcast_in_dim.94
  246.9 117.3 %while.18 = (s32[]{:T(128)}, f32[2,28,20,640]{3,2,1,0:T(8,128)}, f32[5,31,160]{2,1,0:T(8,128)S(1)}, bf16[4,32,5,128]{3,1,2,0:T(8,128)(2,1)}, s32[4]{0:T(128)S(1)...) while((s32[]{:T(128)}, f32[2,28,20,640]{3,2,1,0:T(8,128)}, ...), condition=%wide.region_4.5_spmd.clone, body=%wide.region_0.0_spmd.clone.sunk | while | flops 67648624 | bytes 32509632 | solution.py:184
  258.6 1.3 constant_dynamic-slice_fusion.7
  260.8 1.9 dynamic-slice_bitcast_fusion.5
  266.9 1.2 stack.66
  269.0 1.2 stack.67
  273.2 3.1 fusion.106
  287.9 1.3 constant_dynamic-slice_fusion.7
  290.1 1.9 dynamic-slice_bitcast_fusion.5
  296.2 1.2 stack.66
  298.3 1.2 stack.67
  302.5 3.1 fusion.106
  317.2 1.3 constant_dynamic-slice_fusion.7
  319.4 1.9 dynamic-slice_bitcast_fusion.5
  325.5 1.2 stack.66
  327.6 1.2 stack.67
  331.7 3.1 fusion.106
  346.5 1.3 constant_dynamic-slice_fusion.7
  348.7 1.9 dynamic-slice_bitcast_fusion.5
  354.9 1.2 stack.66
  356.9 1.2 stack.67
  361.1 3.1 fusion.106
  364.2 2.2 convert.16
  366.6 1.1 copy.70
  367.7 1.1 copy.71
  368.8 2.0 collective-permute-start.4
  372.5 155.3 %gather_fusion.2 = f32[13000]{0:T(1024)S(1)} fusion(f32[5,25,8,20]{3,2,1,0:T(8,128)S(1)} %reshape.333, s32[13000]{0:T(1024)S(1)} %reshape.350), kind=kCustom, calls=%fused_computation.2 | custom fusion | bytes 312000 | tf_op jit(solution)/shard_map/jit(take_along_axis)/gather | solution.py:197
  528.2 1.1 copy.73
  529.3 1.1 copy.72
  531.1 2.4 fusion.59
  533.5 1.9 collective-permute-start.6
  535.4 3.7 collective-permute-start.7
  539.3 55.0 %psum.14 = f32[5,25,13]{2,1,0:T(8,128)S(1)} all-reduce(f32[5,25,13]{2,1,0:T(8,128)S(1)} %select_reduce_fusion), channel_id=1, replica_groups=mesh['lat'=8,'lon'=8,'chan'=4] {'lon'}, use_global_device_ids=true, to_apply=%region_7.8 | all-reduce | flops 1625 | bytes 13000 | tf_op jit(solution)/shard_map/psum | solution.py:198
  594.3 34.5 %psum.15 = f32[5,25,13]{2,1,0:T(8,128)S(1)} all-reduce(f32[5,25,13]{2,1,0:T(8,128)S(1)} %psum.14), channel_id=1, replica_groups=mesh['lat'=8,'lon'=8,'chan'=4] {'lat'}, use_global_device_ids=true, to_apply=%region_8.9 | all-reduce | flops 1625 | bytes 13000 | tf_op jit(solution)/shard_map/psum | solution.py:198
  630.6 78.8 %reduce-scatter.2.cloned.1.call-done = f32[80,640]{1,0:T(8,128)} async-done(((f32[5120,640]{1,0:T(8,128)}), f32[80,640]{1,0:T(8,128)}) %reduce-scatter.2.cloned.1.call-update) | async-done | bytes 204816 | tf_op jit(solution)/shard_map/reduce_scatter | solution.py:204
  (282 shorter events, 59.2 us)
Async XLA Ops:
  7.2 29.5 %copy-start = (bf16[16,8,640]{2,1,0:T(8,128)(2,1)S(1)}, bf16[16,8,640]{2,1,0:T(8,128)(2,1)}, u32[]{:S(2)}) copy-start(bf16[16,8,640]{2,1,0:T(8,128)(2,1)} %param.13) | copy-start | bytes 491524
  7.2 29.5 %all-gather.3.cloned.1.call-start = ((), (), s32[]{:S(2)}) async-start(), calls=%async_computation.1 | async-start | bytes 1638400 | tf_op jit(solution)/shard_map/all_gather | solution.py:79
  9.0 231.4 %all-gather.5.cloned.1.call-start = ((), (), s32[]{:S(2)}) async-start(), calls=%async_computation.2 | async-start | bytes 6656000 | tf_op jit(solution)/shard_map/all_gather | solution.py:84
  9.8 699.7 %reduce-scatter.2.cloned.1.call-start = ((), (), s32[]{:S(2)}) async-start(), calls=%async_computation.3 | async-start | bytes 13312000 | tf_op jit(solution)/shard_map/reduce_scatter | solution.py:204
  44.7 0.9 copy-start.9
  44.7 1.0 copy-start.10
  44.7 3.0 copy-start.8
  45.7 4.4 collective-permute-start
  45.8 4.8 collective-permute-start.1
  50.6 5.5 copy-start.1
  51.5 18.9 %collective-permute-start.3 = (bf16[2,28,6,640]{3,0,2,1:T(2,128)(2,1)S(1)}, bf16[2,28,6,640]{3,0,2,1:T(2,128)(2,1)S(1)}, u32[]{:S(2)}, u32[]{:S(2)}) collective-permute-start(bf16[2,28,6,640]{3,0,2,1:T(2,128)(2,1)S(1)} %copy.59), channel_id=1, source_target_pairs={{4,0},{8,4},{12,8},{16,12},{20,16},{24,20},{28,24},{0,28},{5,1},{9... | collective-permute-start | bytes 1290248 | tf_op jit(solution)/shard_map/ppermute | solution.py:18
  56.1 24.8 %collective-permute-start.2 = (bf16[2,28,6,640]{3,0,2,1:T(2,128)(2,1)S(1)}, bf16[2,28,6,640]{3,0,2,1:T(2,128)(2,1)S(1)}, u32[]{:S(2)}, u32[]{:S(2)}) collective-permute-start(bf16[2,28,6,640]{3,0,2,1:T(2,128)(2,1)S(1)} %copy.58), channel_id=1, source_target_pairs={{0,4},{4,8},{8,12},{12,16},{16,20},{20,24},{24,28},{28,0},{1,5},{5... | collective-permute-start | bytes 1290248 | tf_op jit(solution)/shard_map/ppermute | solution.py:17
  81.0 159.4 %copy-start.11 = (bf16[16,8,5120]{2,0,1:T(8,128)(2,1)S(1)}, bf16[16,8,5120]{2,0,1:T(8,128)(2,1)}, u32[]{:S(2)}) copy-start(bf16[16,8,5120]{2,0,1:T(8,128)(2,1)} %all-gather.3.cloned.1.call-done) | copy-start | bytes 3932164
  246.9 13.4 %copy-start.12 = (bf16[16,8,5,128]{3,1,2,0:T(8,128)(2,1)}, bf16[16,8,5,128]{3,1,2,0:T(8,128)(2,1)S(1)}, u32[]{:S(2)}) copy-start(bf16[16,8,5,128]{3,1,2,0:T(8,128)(2,1)S(1)} %get-tuple-element.541) | copy-start | bytes 491524 | tf_op jit(solution)/shard_map/while
  271.5 1.5 copy-start.2
  271.9 1.3 copy-start.3
  273.2 3.1 copy-start.13
  276.2 13.4 %copy-start.12 = (bf16[16,8,5,128]{3,1,2,0:T(8,128)(2,1)}, bf16[16,8,5,128]{3,1,2,0:T(8,128)(2,1)S(1)}, u32[]{:S(2)}) copy-start(bf16[16,8,5,128]{3,1,2,0:T(8,128)(2,1)S(1)} %get-tuple-element.541) | copy-start | bytes 491524 | tf_op jit(solution)/shard_map/while
  300.8 1.5 copy-start.2
  301.2 1.3 copy-start.3
  302.4 3.1 copy-start.13
  305.5 13.4 %copy-start.12 = (bf16[16,8,5,128]{3,1,2,0:T(8,128)(2,1)}, bf16[16,8,5,128]{3,1,2,0:T(8,128)(2,1)S(1)}, u32[]{:S(2)}) copy-start(bf16[16,8,5,128]{3,1,2,0:T(8,128)(2,1)S(1)} %get-tuple-element.541) | copy-start | bytes 491524 | tf_op jit(solution)/shard_map/while
  330.1 1.5 copy-start.2
  330.5 1.3 copy-start.3
  331.7 3.1 copy-start.13
  334.8 13.4 %copy-start.12 = (bf16[16,8,5,128]{3,1,2,0:T(8,128)(2,1)}, bf16[16,8,5,128]{3,1,2,0:T(8,128)(2,1)S(1)}, u32[]{:S(2)}) copy-start(bf16[16,8,5,128]{3,1,2,0:T(8,128)(2,1)S(1)} %get-tuple-element.541) | copy-start | bytes 491524 | tf_op jit(solution)/shard_map/while
  359.4 1.5 copy-start.2
  359.8 1.3 copy-start.3
  361.1 3.1 copy-start.13
  366.5 4.3 copy-start.4
  366.5 4.3 copy-start.6
  366.5 4.7 copy-start.14
  368.8 159.4 %collective-permute-start.5 = (bf16[2,28,6,640]{3,0,2,1:T(2,128)(2,1)}, bf16[2,28,6,640]{3,0,2,1:T(2,128)(2,1)}, u32[]{:S(2)}, u32[]{:S(2)}) collective-permute-start(bf16[2,28,6,640]{3,0,2,1:T(2,128)(2,1)} %copy.71), channel_id=1, source_target_pairs={{4,0},{8,4},{12,8},{16,12},{20,16},{24,20},{28,24},{0,28},{5,1},{9... | collective-permute-start | bytes 1290248 | tf_op jit(solution)/shard_map/ppermute | solution.py:18
  368.8 160.5 %collective-permute-start.4 = (bf16[2,28,6,640]{3,0,2,1:T(2,128)(2,1)}, bf16[2,28,6,640]{3,0,2,1:T(2,128)(2,1)}, u32[]{:S(2)}, u32[]{:S(2)}) collective-permute-start(bf16[2,28,6,640]{3,0,2,1:T(2,128)(2,1)} %copy.70), channel_id=1, source_target_pairs={{0,4},{4,8},{8,12},{12,16},{16,20},{20,24},{24,28},{28,0},{1,5},{5... | collective-permute-start | bytes 1290248 | tf_op jit(solution)/shard_map/ppermute | solution.py:17
  370.8 1.7 copy-start.19
  370.8 1.7 copy-start.15
  370.8 1.7 copy-start.17
  527.8 2.6 copy-start.5
  527.8 2.6 copy-start.7
  530.4 0.7 copy-start.21
  531.1 8.0 %copy-start.16 = (s32[8,13]{1,0:T(8,128)S(1)}, s32[8,13]{1,0:T(8,128)}, u32[]{:S(2)}) copy-start(s32[8,13]{1,0:T(8,128)} %copy-done.15) | copy-start | bytes 1252
  531.1 8.0 %copy-start.18 = (s32[8,13]{1,0:T(8,128)S(1)}, s32[8,13]{1,0:T(8,128)}, u32[]{:S(2)}) copy-start(s32[8,13]{1,0:T(8,128)} %copy-done.17) | copy-start | bytes 1252
  531.1 8.1 %copy-start.20 = (pred[8,13]{1,0:T(8,128)(4,1)S(1)}, pred[8,13]{1,0:T(8,128)(4,1)}, u32[]{:S(2)}) copy-start(pred[8,13]{1,0:T(8,128)(4,1)} %copy-done.19) | copy-start | bytes 316
  533.5 96.2 %copy-start.22 = (pred[16]{0:T(512)(128)(4,1)S(1)}, pred[16]{0:T(512)(128)(4,1)}, u32[]{:S(2)}) copy-start(pred[16]{0:T(512)(128)(4,1)} %constant.227.clone.1) | copy-start | bytes 52
  533.5 96.1 %collective-permute-start.6 = (bf16[2,6,8,640]{3,2,1,0:T(8,128)(2,1)S(1)}, bf16[2,6,8,640]{3,2,1,0:T(8,128)(2,1)S(1)}, u32[]{:S(2)}, u32[]{:S(2)}) collective-permute-start(bf16[2,6,8,640]{3,2,1,0:T(8,128)(2,1)S(1)} %get-tuple-element.361), channel_id=1, source_target_pairs={{0,32},{32,64},{64,96},{96,128},{128,160},{160,192},{192,224},{1,3... | collective-permute-start | bytes 368648 | tf_op jit(solution)/shard_map/ppermute | solution.py:17
  535.4 94.2 %collective-permute-start.7 = (bf16[2,6,8,640]{3,2,1,0:T(8,128)(2,1)S(1)}, bf16[2,6,8,640]{3,2,1,0:T(8,128)(2,1)S(1)}, u32[]{:S(2)}, u32[]{:S(2)}) collective-permute-start(bf16[2,6,8,640]{3,2,1,0:T(8,128)(2,1)S(1)} %get-tuple-element.362), channel_id=1, source_target_pairs={{32,0},{64,32},{96,64},{128,96},{160,128},{192,160},{224,192},{33,... | collective-permute-start | bytes 368648 | tf_op jit(solution)/shard_map/ppermute | solution.py:18
Sparse Core Ops, SparseCore 0:
  9.8 26.8 all-gather.2
  38.5 201.8 all-gather.4
  243.5 465.8 reduce-scatter.1
